TPU v7x, 32 devices: a whole 2x2x4 slice. The times are simulated.
32 devices in a mesh: grp: 8 (over z, y), tp: 2 (over core), fs: 2 (over x).
Axes of the slice: x: 2, y: 2, z: 4, core: 2. Of those that a mesh axis runs over, the one named last changes fastest.
Arguments:
- tokens: bfloat16 [512, 4, 8192], P('grp', None, ('tp', 'fs')), may hold values from -64 to 64
- norm_gain: bfloat16 [8192], P(('tp', 'fs')), may hold values from 0.25 to 1.75
- queries: bfloat16 [512, 4, 8192], P('grp', None, ('tp', 'fs')), may hold values from -64 to 64
- rotated_key_cache: bfloat16 [512, 32, 1024], P('grp', None, ('tp', 'fs')), may hold values from -6 to 6
- head_value_cache: bfloat16 [512, 32, 1024], P('grp', None, ('tp', 'fs')), may hold values from -6 to 6
- lengths: int32 [512], P('grp'), may hold values from 2 to 32
- master: float32 [8192, 2048], P('grp', ('tp', 'fs')), may hold values from -0.0625 to 0.0625
- moment_first: float32 [8192, 2048], P('grp', ('tp', 'fs')), may hold values from -4 to 4
- moment_second: float32 [8192, 2048], P('grp', ('tp', 'fs')), may hold values from 0.1 to 1
- gradient: float32 [8192, 2048], P('grp', ('tp', 'fs')), may hold values from -6 to 6
Outputs:
- attended: bfloat16 [512, 4, 8192], P('grp', None, ('tp', 'fs'))
- appended: bfloat16 [512, 4, 2048], P('grp', None, ('tp', 'fs'))
- new_master: float32 [8192, 2048], P('grp', ('tp', 'fs'))
- new_first: float32 [8192, 2048], P('grp', ('tp', 'fs'))
- new_second: float32 [8192, 2048], P('grp', ('tp', 'fs'))
All inputs are finite; a program needn't handle non-finite values.
Results may differ from a plain program's by a relative error of at most 0.0057.
Values may be sent and summed in bfloat16 or wider, within the bound.
A program may use at most 128 MiB of HBM per device.

v0:
```python
import jax
import jax.numpy as jnp
from jax import lax
from jax.sharding import PartitionSpec as P

MODEL_WIDTH = 8192
QUERY_HEADS = 64
KEY_VALUE_HEADS = 8
HEAD_SIZE = 128
beta_first = 0.9
beta_second = 0.999
correct_first = 0.9999734386011124
correct_second = 0.09520785288629038
adam_eps = 1e-08
learn_rate = 0.003
decay_rate = 0.1
norm_eps = 1e-06
rope_base = 1000000.0


def rotate(keys, positions):
    halfway = keys.shape[-1] // 2
    frequency = rope_base ** (-(jnp.arange(halfway, dtype=jnp.float32) * 2.0 / keys.shape[-1]))
    angles = positions[:, :, None] * frequency[None, None, :]
    cosine = jnp.cos(angles)[:, :, None, :]
    sine = jnp.sin(angles)[:, :, None, :]
    first_half = keys[..., :halfway]
    second_half = keys[..., halfway:]
    return jnp.concatenate(
        [first_half * cosine - second_half * sine, second_half * cosine + first_half * sine],
        axis=-1,
    )


def attention(queries, rotated_key_cache, head_value_cache, key_new, value_new, lengths):
    batch_rows, steps = (queries.shape[0], queries.shape[1])
    window = rotated_key_cache.shape[1]
    kv_heads = rotated_key_cache.shape[2] // HEAD_SIZE
    sharing_factor = QUERY_HEADS // KEY_VALUE_HEADS
    factor = HEAD_SIZE ** (-0.5)
    query_heads = queries.reshape(batch_rows, steps, kv_heads, sharing_factor, HEAD_SIZE)
    cache_key_seeds = rotated_key_cache.reshape(batch_rows, window, kv_heads, HEAD_SIZE)
    cache_values = head_value_cache.reshape(batch_rows, window, kv_heads, HEAD_SIZE)
    scores_cached = (
        jnp.einsum(
            "rsxgd,rlxd->rxgsl", query_heads, cache_key_seeds, preferred_element_type=jnp.float32
        )
        * factor
    )
    scores_fresh = (
        jnp.einsum("rsxgd,ruxd->rxgsu", query_heads, key_new, preferred_element_type=jnp.float32)
        * factor
    )
    present = (jnp.arange(window, dtype=jnp.int32)[None, :] < lengths[:, None])[
        :, None, None, None, :
    ]
    causal = (
        jnp.arange(steps, dtype=jnp.int32)[None, :] <= jnp.arange(steps, dtype=jnp.int32)[:, None]
    )[None, None, None, :, :]
    scores_cached = jnp.where(present, scores_cached, -jnp.inf)
    scores_fresh = jnp.where(causal, scores_fresh, -jnp.inf)
    ceiling = jnp.maximum(
        jnp.max(scores_cached, axis=-1, keepdims=True),
        jnp.max(scores_fresh, axis=-1, keepdims=True),
    )
    probs_cached = jnp.exp(scores_cached - ceiling)
    probs_fresh = jnp.exp(scores_fresh - ceiling)
    denom = jnp.sum(probs_cached, axis=-1, keepdims=True) + jnp.sum(
        probs_fresh, axis=-1, keepdims=True
    )
    weights_cached = probs_cached.astype(jnp.bfloat16)
    weights_fresh = probs_fresh.astype(jnp.bfloat16)
    blended = jnp.einsum(
        "rxgsl,rlxd->rsxgd", weights_cached, cache_values, preferred_element_type=jnp.float32
    )
    blended = blended + jnp.einsum(
        "rxgsu,ruxd->rsxgd", weights_fresh, value_new, preferred_element_type=jnp.float32
    )
    blended = blended / jnp.transpose(denom, (0, 3, 1, 2, 4))
    return blended.astype(jnp.bfloat16).reshape(
        batch_rows, steps, kv_heads * sharing_factor * HEAD_SIZE
    )


def shards(
    tokens,
    norm_gain,
    queries,
    rotated_key_cache,
    head_value_cache,
    lengths,
    master,
    moment_first,
    moment_second,
    gradient,
):
    average = beta_first * moment_first + (1.0 - beta_first) * gradient
    variance = beta_second * moment_second + (1.0 - beta_second) * gradient * gradient
    update = average / correct_first / (jnp.sqrt(variance / correct_second) + adam_eps)
    renewed = master - learn_rate * (update + decay_rate * master)
    layer_half = renewed.astype(jnp.bfloat16)
    widened, gain_whole = (
        lax.all_gather(tokens, ("tp", "fs"), axis=2, tiled=True),
        lax.all_gather(norm_gain, ("tp", "fs"), axis=0, tiled=True),
    )
    mean_square = (
        jnp.einsum("rsd,rsd->rs", widened, widened, preferred_element_type=jnp.float32)[..., None]
        / MODEL_WIDTH
    )
    normed = (widened * lax.rsqrt(mean_square + norm_eps) * gain_whole.astype(jnp.float32)).astype(
        jnp.bfloat16
    )
    batch_rows, steps = (tokens.shape[0], tokens.shape[1])
    flattened = normed.reshape(batch_rows * steps, MODEL_WIDTH)
    columns = layer_half.shape[1]
    gathered = lax.all_gather(layer_half, "grp", axis=0, tiled=True)
    projected_output = jnp.dot(flattened, gathered, preferred_element_type=jnp.float32)
    kv_heads = columns // (2 * HEAD_SIZE)
    projected_output = projected_output.reshape(batch_rows, steps, kv_heads, 2, HEAD_SIZE)
    positions = (lengths[:, None] + jnp.arange(steps, dtype=jnp.int32)[None, :]).astype(jnp.float32)
    key_new = rotate(projected_output[:, :, :, 0, :], positions).astype(jnp.bfloat16)
    value_new = projected_output[:, :, :, 1, :].astype(jnp.bfloat16)
    appended = jnp.stack([key_new, value_new], axis=3).reshape(batch_rows, steps, columns)
    attended = attention(queries, rotated_key_cache, head_value_cache, key_new, value_new, lengths)
    return (attended, appended, renewed, average, variance)


def solution(mesh):
    in_specs = (
        P("grp", None, ("tp", "fs")),
        P(("tp", "fs")),
        P("grp", None, ("tp", "fs")),
        P("grp", None, ("tp", "fs")),
        P("grp", None, ("tp", "fs")),
        P("grp"),
        P("grp", ("tp", "fs")),
        P("grp", ("tp", "fs")),
        P("grp", ("tp", "fs")),
        P("grp", ("tp", "fs")),
    )
    out_specs = (
        P("grp", None, ("tp", "fs")),
        P("grp", None, ("tp", "fs")),
        P("grp", ("tp", "fs")),
        P("grp", ("tp", "fs")),
        P("grp", ("tp", "fs")),
    )
    return jax.shard_map(shards, mesh=mesh, in_specs=in_specs, out_specs=out_specs, check_vma=False)
```

profile of v0, /device:TPU:0, one launch (start us, length us, event | category | flops | bytes accessed | tf_op | source)
XLA Modules:
  0.0 219.5 jit_solution(13725057092368029306)
XLA Ops:
  7.2 0.0 all-gather.3.cloned.1.call-start
  7.2 0.7 all-gather.3.cloned.1.call-update
  7.9 0.0 copy-start.6
  7.9 0.0 copy-start.1
  7.9 0.0 all-gather.5.cloned.1.call-start
  8.0 7.8 %fusion.33 = (bf16[1024,512]{1,0:T(8,128)(2,1)}, f32[1024,512]{1,0:T(8,128)}, f32[1024,512]{1,0:T(8,128)}, f32[1024,512]{1,0:T(8,128)}) fusion(f32[1024,512]{1,0:T(8,128)} %param.16, f32[1024,512]{1,0:T(8,128)} %param.19, f32[1024,512]{1,0:T(8,128)} %param.17, f32[1024,512]{1,0:T(8,128)} %param.18), kind=kLoop, calls=%fused_computation.56 | loop fusion | flops 8388608 | bytes 15728640 | tf_op jit(solution)/shard_map/convert_element_type | solution.py:101
  15.8 0.0 copy-start.2
  15.8 0.0 all-gather.5.cloned.1.call-update
  15.8 0.0 copy-done.6
  15.8 10.8 %all_gather.10 = bf16[8192]{0:T(1024)(128)(2,1)S(1)} all-gather(bf16[2048]{0:T(1024)(128)(2,1)S(1)} %copy-done.6), channel_id=1, replica_groups=mesh['grp'=8,'tp'=2,'fs'=2] {'tp','fs'}, dimensions={0}, use_global_device_ids=true | all-gather | bytes 20480 | tf_op jit(solution)/shard_map/all_gather | solution.py:104
  26.7 0.0 copy-done.1
  26.7 0.0 copy-start.3
  26.7 1.5 reshape.145
  28.2 0.0 copy-done.2
  28.2 0.0 copy-start.7
  28.2 1.1 reshape.144
  29.3 0.0 copy-done.3
  29.3 1.1 reshape.146
  30.4 0.0 copy-done.7
  30.4 0.1 iota_compare_fusion
  30.5 0.5 multiply_cosine_fusion
  31.0 2.4 %bitcast_reduce_fusion = (f32[64,2,8,4]{2,3,1,0:T(4,128)S(1)}, f32[64,2,32,4,8]{2,4,3,1,0:T(8,128)S(1)}) fusion(pred[64,32]{1,0:T(8,128)(4,1)S(1)} %iota_compare_fusion, bf16[64,4,2,8,128]{4,3,2,1,0:T(8,128)(2,1)} %reshape.145, bf16[64,32,2,128,1]{3,2,1,0,4:T(2,128)(2,1)} %bitcast.58), kind=kOutput, calls=%fused_computation.14 | convolution fusion | flops 33943552 | bytes 2639872 | tf_op jit(solution)/shard_map/rsxgd,rlxd->rxgsl/dot_general | solution.py:45
  33.4 13.5 %all-gather.3.cloned.1.call-done = bf16[64,4,8192]{2,1,0:T(4,128)(2,1)} async-done(((bf16[64,4,2048]{2,1,0:T(4,128)(2,1)}), bf16[64,4,8192]{2,1,0:T(4,128)(2,1)}) %all-gather.3.cloned.1.call-update) | async-done | bytes 4194320 | tf_op jit(solution)/shard_map/all_gather | solution.py:103
  46.9 0.0 copy-start
  46.9 4.6 %fusion.2 = f32[64,4]{1,0:T(8,128)S(1)} fusion(bf16[64,4,8192]{2,1,0:T(4,128)(2,1)} %all-gather.3.cloned.1.call-done), kind=kLoop, calls=%fused_computation.4 | loop fusion | flops 6291200 | bytes 4195328 | tf_op jit(solution)/shard_map/rsd,rsd->rs/dot_general | solution.py:107
  51.5 0.0 copy-done
  51.5 4.7 %fusion.3 = bf16[64,4,8192,1,1]{2,1,0,4,3:T(4,128)(2,1)} fusion(bf16[64,4,8192]{2,1,0:T(4,128)(2,1)S(1)} %copy-done, f32[8192]{0:T(1024)S(1)} %convert_element_type.44, f32[64,4]{1,0:T(8,128)S(1)} %add_rsqrt_fusion), kind=kLoop, calls=%fused_computation.5 | loop fusion | flops 8388608 | bytes 8422400 | tf_op jit(solution)/shard_map/convert_element_type | solution.py:110
  56.3 117.3 %all-gather.5.cloned.1.call-done = bf16[8192,512]{1,0:T(8,128)(2,1)} async-done(((bf16[1024,512]{1,0:T(8,128)(2,1)}), bf16[8192,512]{1,0:T(8,128)(2,1)}) %all-gather.5.cloned.1.call-update) | async-done | bytes 8388624 | tf_op jit(solution)/shard_map/all_gather | solution.py:116
  173.6 11.9 %copy.41 = bf16[512,8192]{1,0:T(8,128)(2,1)} copy(bf16[512,8192]{0,1:T(8,128)(2,1)} %bitcast.53) | data formatting | bytes 16777216 | tf_op jit(solution)/shard_map/dot_general | solution.py:117
  185.5 13.5 %fusion.4 = f32[64,4,2,2,128]{4,0,3,2,1:T(8,128)S(1)} fusion(bf16[2,2,128,8192,1]{3,2,1,0,4:T(8,128)(2,1)} %bitcast.54, bf16[64,4,8192,1,1]{2,1,0,4,3:T(4,128)(2,1)} %fusion.3), kind=kOutput, calls=%fused_computation.6 | convolution fusion | flops 2147483648 | bytes 13107200 | tf_op jit(solution)/shard_map/dot_general | solution.py:117
  199.0 0.0 copy-start.5
  199.1 0.2 subtract_convert_fusion
  199.3 0.1 maximum_bitcast_fusion
  199.4 0.9 copy-done.5
  200.3 4.7 %fusion.35 = (f32[64,2,8,4]{2,3,1,0:T(4,128)S(1)}, f32[64,2,8,4,4]{2,4,3,1,0:T(4,128)S(1)}) fusion(bf16[64,4,2,8,128]{4,3,2,1,0:T(8,128)(2,1)S(1)} %copy-done.5, bf16[64,4,2,128,1]{3,0,2,1,4:T(8,128)(2,1)S(1)} %maximum_bitcast_fusion, pred[4,4]{1,0:T(4,128)(4,1)S(1)} %iota_compare_fusion.1), kind=kOutput, calls=%fused_computation.57 | convolution fusion | flops 4239360 | bytes 1261584 | tf_op jit(solution)/shard_map/rsxgd,ruxd->rxgsu/dot_general | solution.py:51
  205.0 0.1 max.8
  205.1 0.0 copy-start.4
  205.1 1.0 fusion.25
  206.0 1.4 fusion.10
  207.5 0.0 copy-done.4
  207.5 1.4 fusion.14
  208.8 0.1 add_bitcast_fusion
  208.9 1.2 fusion.8
  210.1 0.2 copy.72
  210.3 1.1 reshape.157
  211.4 0.1 pad_maximum_fusion
  211.6 0.3 copy.73
  211.8 0.8 reshape.158
  (8 shorter events, 0.1 us)
Async XLA Ops:
  7.2 39.8 %all-gather.3.cloned.1.call-start = ((), (), s32[]{:S(2)}) async-start(), calls=%async_computation | async-start | bytes 5242880 | tf_op jit(solution)/shard_map/all_gather | solution.py:103
  7.9 7.9 %copy-start.6 = (bf16[2048]{0:T(1024)(128)(2,1)S(1)}, bf16[2048]{0:T(1024)(128)(2,1)}, u32[]{:S(2)}) copy-start(bf16[2048]{0:T(1024)(128)(2,1)} %param.11) | copy-start | bytes 12292
  7.9 18.8 %copy-start.1 = (bf16[64,4,2048]{2,1,0:T(4,128)(2,1)S(1)}, bf16[64,4,2048]{2,1,0:T(4,128)(2,1)}, u32[]{:S(2)}) copy-start(bf16[64,4,2048]{2,1,0:T(4,128)(2,1)} %param.12) | copy-start | bytes 3145732
  7.9 165.7 %all-gather.5.cloned.1.call-start = ((), (), s32[]{:S(2)}) async-start(), calls=%async_computation.1 | async-start | bytes 9437184 | tf_op jit(solution)/shard_map/all_gather | solution.py:116
  15.8 12.4 %copy-start.2 = (bf16[64,32,256]{2,1,0:T(8,128)(2,1)S(1)}, bf16[64,32,256]{2,1,0:T(8,128)(2,1)}, u32[]{:S(2)}) copy-start(bf16[64,32,256]{2,1,0:T(8,128)(2,1)} %param.13) | copy-start | bytes 3145732
  26.7 2.6 %copy-start.3 = (bf16[64,32,256]{2,1,0:T(8,128)(2,1)S(1)}, bf16[64,32,256]{2,1,0:T(8,128)(2,1)}, u32[]{:S(2)}) copy-start(bf16[64,32,256]{2,1,0:T(8,128)(2,1)} %param.14) | copy-start | bytes 3145732
  28.2 2.2 %copy-start.7 = (s32[64]{0:T(128)S(1)}, s32[64]{0:T(128)}, u32[]{:S(2)}) copy-start(s32[64]{0:T(128)} %param.15) | copy-start | bytes 772
  46.9 4.6 %copy-start = (bf16[64,4,8192]{2,1,0:T(4,128)(2,1)S(1)}, bf16[64,4,8192]{2,1,0:T(4,128)(2,1)}, u32[]{:S(2)}) copy-start(bf16[64,4,8192]{2,1,0:T(4,128)(2,1)} %all-gather.3.cloned.1.call-done) | copy-start | bytes 12582916
  199.0 1.2 copy-start.5
  205.1 2.4 %copy-start.4 = (bf16[64,32,2,128]{3,2,1,0:T(2,128)(2,1)S(1)}, bf16[64,32,2,128]{3,2,1,0:T(2,128)(2,1)}, u32[]{:S(2)}) copy-start(bf16[64,32,2,128]{3,2,1,0:T(2,128)(2,1)} %reshape.146) | copy-start | bytes 3145732
Sparse Core Ops, SparseCore 0:
  9.5 37.3 all-gather.2
  49.0 124.5 all-gather.4
where the time goes:
time: 220 us; the launch traced here: 219 us
  waiting for transfers between devices  132 us (60%)
  matrix products  23.2 us (11%)
  other arithmetic  20.7 us (9%)
  local copies, waits for them, and re-layouts  18.9 us (9%)
  between operations  14.2 us (6%)
  blocking collectives  10.8 us (5%)
    all_gather x1, waiting for transfers between devices, shards(): gathered = lax.all_gather(layer_half, 'grp', axis=0, tiled=True)  117 us
    dot_general x1, matrix products, shards(): jnp.dot(flattened, gathered, preferred_element_type=jnp.float32)  13.5 us
    all_gather x1, waiting for transfers between devices, shards(): lax.all_gather(tokens, ('tp', 'fs'), axis=2, tiled=True)  13.5 us
    dot_general x1, local copies, waits for them, and re-layouts, shards(): jnp.dot(flattened, gathered, preferred_element_type=jnp.float32)  11.9 us
    all_gather x1, blocking collectives, shards(): lax.all_gather(norm_gain, ('tp', 'fs'), axis=0, tiled=True)  10.8 us
    convert_element_type x1, other arithmetic, shards(): layer_half = renewed.astype(jnp.bfloat16)  7.82 us
    dot_general x1, matrix products, attention(): jnp.einsum('rsxgd,ruxd->rxgsu', query_heads, key_new, preferred_element_t...  4.73 us
    convert_element_type x1, other arithmetic, shards(): (widened * lax.rsqrt(mean_square + norm_eps) * gain_whole.astype(jnp.floa...  4.72 us
  transfers between devices with their start and end apart: 2, of which 2 were waited for; matrix products, arithmetic and copies ran while one was open for 11% of the time, Pallas kernels for 0%

commit v1 on v0

--- a/solution.py
+++ b/solution.py
@@ -100,7 +100,7 @@
     renewed = master - learn_rate * (update + decay_rate * master)
     layer_half = renewed.astype(jnp.bfloat16)
     widened, gain_whole = (
-        lax.all_gather(tokens, ("tp", "fs"), axis=2, tiled=True),
+        jnp.concatenate(lax.all_gather(tokens, ("tp", "fs")), axis=2),
         lax.all_gather(norm_gain, ("tp", "fs"), axis=0, tiled=True),
     )
     mean_square = (

time: 220 us -> 213 us (0.968)
  waiting for transfers between devices: 132 us -> 104 us
  local copies, waits for them, and re-layouts: 18.9 us -> 42.3 us
  matrix products: 23.2 us -> 15.9 us
  other arithmetic: 20.7 us -> 24.4 us
    all_gather x1, waiting for transfers between devices: 117 us -> 90.3 us  [shards(): gathered = lax.all_gather(layer_half, 'grp', axis=0, tiled=True)]
    reshape x0 -> x1, local copies, waits for them, and re-layouts: none -> 7.92 us  [shards(): jnp.concatenate(lax.all_gather(tokens, ('tp', 'fs')), axis=2)]
    convert_element_type x0 -> x1, local copies, waits for them, and re-layouts: none -> 7.75 us  [shards(): (widened * lax.rsqrt(mean_square + norm_eps) * gain_whole.astype(jnp.floa...]
    all_gather x0 -> x1, local copies, waits for them, and re-layouts: none -> 7.45 us  [shards(): lax.all_gather(tokens, ('tp', 'fs'))]
    dot_general x1, matrix products: 13.5 us -> 6.28 us  [shards(): jnp.dot(flattened, gathered, preferred_element_type=jnp.float32)]
    convert_element_type x1, other arithmetic: 4.72 us -> 9.77 us  [shards(): (widened * lax.rsqrt(mean_square + norm_eps) * gain_whole.astype(jnp.floa...]
  transfers between devices with their start and end apart: 2 -> 2, of which waited for: 2 -> 2; matrix products, arithmetic and copies ran while one was open for 11% -> 24% of each run, Pallas kernels for 0% -> 0%
where the time goes in v1:
time: 213 us; the launch traced here: 212 us
  waiting for transfers between devices  104 us (49%)
  local copies, waits for them, and re-layouts  42.3 us (20%)
  other arithmetic  24.4 us (11%)
  matrix products  15.9 us (7%)
  between operations  14.2 us (7%)
  blocking collectives  11.1 us (5%)
    all_gather x1, waiting for transfers between devices, shards(): gathered = lax.all_gather(layer_half, 'grp', axis=0, tiled=True)  90.3 us
    all_gather x1, waiting for transfers between devices, shards(): lax.all_gather(tokens, ('tp', 'fs'))  13.2 us
    dot_general x1, local copies, waits for them, and re-layouts, shards(): jnp.dot(flattened, gathered, preferred_element_type=jnp.float32)  11.9 us
    all_gather x1, blocking collectives, shards(): lax.all_gather(norm_gain, ('tp', 'fs'), axis=0, tiled=True)  11.1 us
    convert_element_type x1, other arithmetic, shards(): (widened * lax.rsqrt(mean_square + norm_eps) * gain_whole.astype(jnp.floa...  9.77 us
    reshape x1, local copies, waits for them, and re-layouts, shards(): jnp.concatenate(lax.all_gather(tokens, ('tp', 'fs')), axis=2)  7.92 us
    convert_element_type x1, other arithmetic, shards(): layer_half = renewed.astype(jnp.bfloat16)  7.79 us
    convert_element_type x1, local copies, waits for them, and re-layouts, shards(): (widened * lax.rsqrt(mean_square + norm_eps) * gain_whole.astype(jnp.floa...  7.75 us
  transfers between devices with their start and end apart: 2, of which 2 were waited for; matrix products, arithmetic and copies ran while one was open for 24% of the time, Pallas kernels for 0%

profile of v1, /device:TPU:0, one launch (start us, length us, event | category | flops | bytes accessed | tf_op | source)
XLA Modules:
  0.0 212.2 jit_solution(2906579438122613036)
XLA Ops:
  7.2 0.0 all-gather.6.cloned.1.call-start
  7.2 0.7 all-gather.6.cloned.1.call-update
  7.9 0.0 copy-start.6
  7.9 0.0 copy-start.1
  7.9 0.0 all-gather.4.cloned.1.call-start
  8.0 7.8 %fusion.30 = (bf16[1024,512]{1,0:T(8,128)(2,1)}, f32[1024,512]{1,0:T(8,128)}, f32[1024,512]{1,0:T(8,128)}, f32[1024,512]{1,0:T(8,128)}) fusion(f32[1024,512]{1,0:T(8,128)} %param.16, f32[1024,512]{1,0:T(8,128)} %param.19, f32[1024,512]{1,0:T(8,128)} %param.17, f32[1024,512]{1,0:T(8,128)} %param.18), kind=kLoop, calls=%fused_computation.54 | loop fusion | flops 8388608 | bytes 15728640 | tf_op jit(solution)/shard_map/convert_element_type | solution.py:101
  15.8 0.0 copy-start.2
  15.8 0.0 all-gather.4.cloned.1.call-update
  15.8 0.0 copy-done.6
  15.8 11.1 %all_gather.14 = bf16[8192]{0:T(1024)(128)(2,1)S(1)} all-gather(bf16[2048]{0:T(1024)(128)(2,1)S(1)} %copy-done.6), channel_id=1, replica_groups=mesh['grp'=8,'tp'=2,'fs'=2] {'tp','fs'}, dimensions={0}, use_global_device_ids=true | all-gather | bytes 20480 | tf_op jit(solution)/shard_map/all_gather | solution.py:104
  26.9 0.0 copy-done.1
  26.9 0.0 copy-start.3
  26.9 1.5 reshape.175
  28.4 0.0 copy-done.2
  28.4 0.0 copy-start.7
  28.4 1.2 reshape.174
  29.6 0.0 copy-done.3
  29.6 1.1 reshape.178
  30.7 0.0 copy-done.7
  30.7 0.1 iota_compare_fusion
  30.8 0.5 multiply_cosine_fusion
  31.3 2.4 %bitcast_reduce_fusion = (f32[64,2,8,4]{2,3,1,0:T(4,128)S(1)}, f32[64,2,32,4,8]{2,4,3,1,0:T(8,128)S(1)}) fusion(pred[64,32]{1,0:T(8,128)(4,1)S(1)} %iota_compare_fusion, bf16[64,4,2,8,128]{4,3,2,1,0:T(8,128)(2,1)} %reshape.175, bf16[64,32,2,128,1]{3,2,1,0,4:T(2,128)(2,1)} %bitcast.72), kind=kOutput, calls=%fused_computation.12 | convolution fusion | flops 33943552 | bytes 2639872 | tf_op jit(solution)/shard_map/rsxgd,rlxd->rxgsl/dot_general | solution.py:45
  33.7 13.2 %all-gather.6.cloned.1.call-done = bf16[256,4,2048]{2,1,0:T(4,128)(2,1)} async-done(((bf16[64,4,2048]{2,1,0:T(4,128)(2,1)}), bf16[256,4,2048]{2,1,0:T(4,128)(2,1)}) %all-gather.6.cloned.1.call-update) | async-done | bytes 4194320 | tf_op jit(solution)/shard_map/all_gather | solution.py:103
  46.9 7.5 %copy.98 = bf16[4,64,4,2048]{3,0,1,2:T(4,128)(2,1)} copy(bf16[4,64,4,2048]{3,2,1,0:T(4,128)(2,1)} %bitcast.64) | data formatting | bytes 8388608 | tf_op jit(solution)/shard_map/all_gather | solution.py:103
  54.4 7.9 %reshape.177 = bf16[64,4,8192]{2,0,1:T(8,128)(2,1)} reshape(bf16[64,4,4,2048]{3,2,0,1:T(4,128)(2,1)} %bitcast.66) | data formatting | bytes 8388608 | tf_op jit(solution)/shard_map/reshape | solution.py:103
  62.3 0.0 copy-start
  62.3 3.3 %fusion = f32[64,4]{0,1:T(4,128)S(1)} fusion(bf16[64,4,8192]{2,0,1:T(8,128)(2,1)} %reshape.177), kind=kLoop, calls=%fused_computation.1 | loop fusion | flops 6291200 | bytes 4195328 | tf_op jit(solution)/shard_map/rsd,rsd->rs/dot_general | solution.py:107
  65.6 0.2 copy-done
  65.8 9.8 %multiply_convert_fusion = bf16[64,4,4,2048]{3,2,0,1:T(4,128)(2,1)} fusion(f32[4,2048]{1,0:T(4,128)S(1)} %reshape.181, f32[64,4]{0,1:T(4,128)S(1)} %add_rsqrt_fusion, bf16[4,64,4,2048]{3,2,1,0:T(4,128)(2,1)S(1)} %bitcast.65), kind=kLoop, calls=%fused_computation.2 | loop fusion | flops 8388608 | bytes 8422400 | tf_op jit(solution)/shard_map/convert_element_type | solution.py:110
  75.5 7.7 %reshape.186 = bf16[64,4,8192,1,1]{2,0,1,3,4:T(8,128)(2,1)} reshape(bf16[64,4,4,2048]{3,2,0,1:T(4,128)(2,1)} %multiply_convert_fusion) | data formatting | bytes 8388608 | tf_op jit(solution)/shard_map/convert_element_type | solution.py:110
  83.3 90.3 %all-gather.4.cloned.1.call-done = bf16[8192,512]{1,0:T(8,128)(2,1)} async-done(((bf16[1024,512]{1,0:T(8,128)(2,1)}), bf16[8192,512]{1,0:T(8,128)(2,1)}) %all-gather.4.cloned.1.call-update) | async-done | bytes 8388624 | tf_op jit(solution)/shard_map/all_gather | solution.py:116
  173.6 11.9 %copy.42 = bf16[512,8192]{1,0:T(8,128)(2,1)} copy(bf16[512,8192]{0,1:T(8,128)(2,1)} %bitcast.67) | data formatting | bytes 16777216 | tf_op jit(solution)/shard_map/dot_general | solution.py:117
  185.5 6.3 %fusion.1 = f32[64,4,2,2,128]{4,0,3,2,1:T(8,128)S(1)} fusion(bf16[2,2,128,8192,1]{3,2,1,0,4:T(8,128)(2,1)} %bitcast.68, bf16[64,4,8192,1,1]{2,0,1,3,4:T(8,128)(2,1)} %reshape.186), kind=kOutput, calls=%fused_computation.3 | convolution fusion | flops 2147483648 | bytes 13107200 | tf_op jit(solution)/shard_map/dot_general | solution.py:117
  191.8 0.0 copy-start.5
  191.9 0.2 subtract_convert_fusion
  192.0 0.1 maximum_bitcast_fusion
  192.1 0.9 copy-done.5
  193.0 4.7 %fusion.32 = (f32[64,2,8,4]{2,3,1,0:T(4,128)S(1)}, f32[64,2,8,4,4]{2,4,3,1,0:T(4,128)S(1)}) fusion(bf16[64,4,2,8,128]{4,3,2,1,0:T(8,128)(2,1)S(1)} %copy-done.5, bf16[64,4,2,128,1]{3,0,2,1,4:T(8,128)(2,1)S(1)} %maximum_bitcast_fusion, pred[4,4]{1,0:T(4,128)(4,1)S(1)} %iota_compare_fusion.1), kind=kOutput, calls=%fused_computation.55 | convolution fusion | flops 4239360 | bytes 1261584 | tf_op jit(solution)/shard_map/rsxgd,ruxd->rxgsu/dot_general | solution.py:51
  197.7 0.1 max.8
  197.8 0.0 copy-start.4
  197.8 1.0 fusion.22
  198.8 1.4 fusion.7
  200.2 0.0 copy-done.4
  200.2 1.4 fusion.11
  201.6 0.1 add_bitcast_fusion
  201.7 1.2 fusion.5
  202.9 0.2 copy.70
  203.1 1.1 reshape.192
  204.2 0.1 pad_maximum_fusion
  204.3 0.3 copy.71
  204.6 0.8 reshape.193
  (8 shorter events, 0.1 us)
Async XLA Ops:
  7.2 39.8 %all-gather.6.cloned.1.call-start = ((), (), s32[]{:S(2)}) async-start(), calls=%async_computation.1 | async-start | bytes 5242880 | tf_op jit(solution)/shard_map/all_gather | solution.py:103
  7.9 7.9 %copy-start.6 = (bf16[2048]{0:T(1024)(128)(2,1)S(1)}, bf16[2048]{0:T(1024)(128)(2,1)}, u32[]{:S(2)}) copy-start(bf16[2048]{0:T(1024)(128)(2,1)} %param.11) | copy-start | bytes 12292
  7.9 19.0 %copy-start.1 = (bf16[64,4,2048]{2,1,0:T(4,128)(2,1)S(1)}, bf16[64,4,2048]{2,1,0:T(4,128)(2,1)}, u32[]{:S(2)}) copy-start(bf16[64,4,2048]{2,1,0:T(4,128)(2,1)} %param.12) | copy-start | bytes 3145732
  7.9 165.7 %all-gather.4.cloned.1.call-start = ((), (), s32[]{:S(2)}) async-start(), calls=%async_computation | async-start | bytes 9437184 | tf_op jit(solution)/shard_map/all_gather | solution.py:116
  15.8 12.6 %copy-start.2 = (bf16[64,32,256]{2,1,0:T(8,128)(2,1)S(1)}, bf16[64,32,256]{2,1,0:T(8,128)(2,1)}, u32[]{:S(2)}) copy-start(bf16[64,32,256]{2,1,0:T(8,128)(2,1)} %param.13) | copy-start | bytes 3145732
  26.9 2.7 %copy-start.3 = (bf16[64,32,256]{2,1,0:T(8,128)(2,1)S(1)}, bf16[64,32,256]{2,1,0:T(8,128)(2,1)}, u32[]{:S(2)}) copy-start(bf16[64,32,256]{2,1,0:T(8,128)(2,1)} %param.14) | copy-start | bytes 3145732
  28.4 2.3 %copy-start.7 = (s32[64]{0:T(128)S(1)}, s32[64]{0:T(128)}, u32[]{:S(2)}) copy-start(s32[64]{0:T(128)} %param.15) | copy-start | bytes 772
  62.3 3.5 %copy-start = (bf16[256,4,2048]{2,1,0:T(4,128)(2,1)S(1)}, bf16[256,4,2048]{2,1,0:T(4,128)(2,1)}, u32[]{:S(2)}) copy-start(bf16[256,4,2048]{2,1,0:T(4,128)(2,1)} %all-gather.6.cloned.1.call-done) | copy-start | bytes 12582916
  191.8 1.2 copy-start.5
  197.8 2.4 %copy-start.4 = (bf16[64,32,2,128]{3,2,1,0:T(2,128)(2,1)S(1)}, bf16[64,32,2,128]{3,2,1,0:T(2,128)(2,1)}, u32[]{:S(2)}) copy-start(bf16[64,32,2,128]{3,2,1,0:T(2,128)(2,1)} %reshape.178) | copy-start | bytes 3145732
Sparse Core Ops, SparseCore 0:
  9.5 37.3 all-gather.5
  49.0 124.5 all-gather.3
